TPU v7x, 512 devices: a whole 4x4x16 slice. The times are simulated.
512 devices in a mesh: rep: 32 (over z, core), exp: 16 (over y, x).
Axes of the slice: x: 4, y: 4, z: 16, core: 2. Of those that a mesh axis runs over, the one named last changes fastest.
Arguments:
- tokens: bfloat16 [65536, 4096], P(('rep', 'exp')), may hold values from -6 to 6
- grad_out: bfloat16 [65536, 4096], P(('rep', 'exp')), may hold values from -6 to 6
- gates: float32 [65536, 2], P(('rep', 'exp')), may hold values from 0.1 to 0.9
- expert_ids: int32 [65536, 2], P(('rep', 'exp')), may hold values from 0 to 15, all different within a row; in each aligned block of 128 rows (0 to 127, 128 to 255, ...) at most 20 rows name the same one
- w_all: bfloat16 [16, 4096, 384], P('exp', 'rep'), may hold values from -0.09375 to 0.09375
- touched: int32 [32, 16, 32], P('rep', 'exp'), may hold values 0 or 1
Outputs:
- token_grad: bfloat16 [65536, 4096], P(('rep', 'exp'))
- weight_grad: float32 [16, 4096, 384], P('exp', 'rep')
Inputs may be any that keep to these rules, and one draw needn't show every extreme that they name: `expert_ids`: each token names two different experts. Among the tokens of one device no expert is named more than 20 times, a bound that some block reaches.
All inputs are finite; a program needn't handle non-finite values. No bound on the sum of `touched` on one device may be relied on, other than what follows from the above.
Results may differ from a plain program's by a relative error of at most 0.017.
Values may be sent and summed in bfloat16 or wider, within the bound.
No kernel may reach another device: no remote copies, remote signals or barrier semaphores. Data moves between devices by JAX's collectives and lax.ppermute only.
A program may use at most 64 MiB of HBM per device.

v0:
```python
import jax
import jax.numpy as jnp
from jax import lax
from jax.sharding import PartitionSpec as P


def silu_terms(gate_pre):
    sigmoid_g = jax.nn.sigmoid(gate_pre)
    return (gate_pre * sigmoid_g, sigmoid_g * (1.0 + gate_pre * (1.0 - sigmoid_g)))


def contract_rows(left, right):
    return lax.dot_general(
        left, right, (((0,), (0,)), ((), ())), preferred_element_type=jnp.float32
    )


def per_device(tokens, grad_out, gates, expert_ids, w_all, touched):
    tok_count = tokens.shape[0]
    model_width = tokens.shape[1]
    expert_count = lax.axis_size("exp")
    capacity = 5 * tok_count // (2 * expert_count)
    slot_count = expert_count * capacity
    hidden_count = w_all.shape[2] // 3
    flat_ids = expert_ids.reshape(-1)
    onehot = (flat_ids[:, None] == jnp.arange(expert_count, dtype=jnp.int32)[None, :]).astype(
        jnp.int32
    )
    slot_rank = jnp.sum(jnp.cumsum(onehot, 0) * onehot, 1) - 1
    target = flat_ids * capacity + slot_rank
    placed = target[None, :] == jnp.arange(slot_count, dtype=jnp.int32)[:, None]
    place_pair = placed.astype(jnp.bfloat16)
    place_token = jnp.sum(placed.reshape(slot_count, tok_count, 2).astype(jnp.int32), 2).astype(
        jnp.bfloat16
    )
    scaled = (grad_out.astype(jnp.float32)[:, None, :] * gates[:, :, None]).astype(jnp.bfloat16)
    scaled = scaled.reshape(2 * tok_count, model_width)
    send_x = jnp.dot(place_token, tokens, preferred_element_type=jnp.float32).astype(jnp.bfloat16)
    send_dy = jnp.dot(place_pair, scaled, preferred_element_type=jnp.float32).astype(jnp.bfloat16)
    recv_x, recv_dy = (
        lax.all_to_all(
            send_x.reshape(expert_count, capacity, model_width),
            "exp",
            split_axis=0,
            concat_axis=0,
            tiled=True,
        ),
        lax.all_to_all(
            send_dy.reshape(expert_count, capacity, model_width),
            "exp",
            split_axis=0,
            concat_axis=0,
            tiled=True,
        ),
    )
    slot_x = recv_x.reshape(slot_count, model_width)
    slot_dy = recv_dy.reshape(slot_count, model_width)
    w_local = w_all[0]
    w_whole = lax.all_gather(w_local, "rep", axis=0, tiled=True)
    gate_up = jnp.dot(slot_x, w_whole[:, : 2 * hidden_count], preferred_element_type=jnp.float32)
    hid_grad = jnp.dot(slot_dy, w_whole[:, 2 * hidden_count :], preferred_element_type=jnp.float32)
    gate_pre = gate_up[:, :hidden_count]
    up_pre = gate_up[:, hidden_count:]
    silu_val, silu_slope = silu_terms(gate_pre)
    hidden = (silu_val * up_pre).astype(jnp.bfloat16)
    gate_grad = (hid_grad * up_pre * silu_slope).astype(jnp.bfloat16)
    up_grad = (hid_grad * silu_val).astype(jnp.bfloat16)
    both_grad = jnp.concatenate([gate_grad, up_grad], 1)
    row_mask = jnp.repeat(touched[0, 0].astype(jnp.float32), 128)[:, None]
    full_grad = jnp.concatenate(
        [contract_rows(slot_x, both_grad), contract_rows(slot_dy, hidden)], 1
    )
    masked = lax.optimization_barrier((full_grad * row_mask).astype(jnp.bfloat16)).astype(
        jnp.float32
    )
    owned = lax.psum_scatter(
        masked.astype(jnp.bfloat16), "rep", scatter_dimension=0, tiled=True
    ).astype(jnp.float32)
    slot_grad = lax.dot_general(
        both_grad,
        w_whole[:, : 2 * hidden_count],
        (((1,), (1,)), ((), ())),
        preferred_element_type=jnp.float32,
    )
    slot_grad = slot_grad.astype(jnp.bfloat16)
    returned = lax.all_to_all(
        slot_grad.reshape(expert_count, capacity, model_width),
        "exp",
        split_axis=0,
        concat_axis=0,
        tiled=True,
    )
    returned = returned.reshape(slot_count, model_width)
    token_grad = contract_rows(place_token, returned).astype(jnp.bfloat16)
    return (token_grad, owned[None])


def solution(mesh):
    in_specs = (
        P(("rep", "exp"), None),
        P(("rep", "exp"), None),
        P(("rep", "exp"), None),
        P(("rep", "exp"), None),
        P("exp", "rep", None),
        P("rep", "exp", None),
    )
    out_specs = (P(("rep", "exp"), None), P("exp", "rep", None))
    return jax.shard_map(
        per_device, mesh=mesh, in_specs=in_specs, out_specs=out_specs, check_vma=False
    )
```

profile of v0, /device:TPU:2, one launch (start us, length us, event | category | flops | bytes accessed | tf_op | source)
XLA Modules:
  0.0 266.7 jit_solution(8348941351886036165)
XLA Ops:
  7.2 0.0 copy-start
  7.2 0.0 all-gather.3.cloned.1.call-start
  7.2 0.7 all-gather.3.cloned.1.call-update
  7.9 0.8 copy.32
  8.7 0.1 eq.49
  8.9 0.1 eq.45
  9.0 0.6 reduce-window.6
  9.6 0.2 slice_reduce_fusion
  9.8 0.1 fusion.15
  9.9 0.1 sub.10
  10.1 0.1 copy.35
  10.1 0.7 multiply_add_fusion.1
  10.9 0.0 copy-done
  10.9 2.4 convolution_convert_fusion.1
  13.3 4.3 %reshape.72 = bf16[16,20,4096]{2,1,0:T(8,128)(2,1)} reshape(bf16[320,4096]{1,0:T(8,128)(2,1)} %convolution_convert_fusion.1) | data formatting | bytes 5242880 | tf_op jit(solution)/shard_map/reshape | solution.py:42
  17.6 10.2 %all-to-all-start.1 = ((bf16[16,20,4096]{2,1,0:T(8,128)(2,1)}), bf16[16,20,4096]{2,1,0:T(8,128)(2,1)}, u32[]{:S(2)}, u32[]{:S(2)}) async-start(bf16[16,20,4096]{2,1,0:T(8,128)(2,1)} %reshape.72), calls=%async_computation.1 | async-start | bytes 6291456 | tf_op jit(solution)/shard_map/all_to_all | solution.py:41
  27.8 0.0 copy-done.3
  27.8 4.1 %mul.72 = f32[128,2,4096]{2,1,0:T(2,128)} broadcast(bf16[128,4096]{1,0:T(8,128)(2,1)S(1)} %copy-done.3), dimensions={0,2} | broadcast | bytes 5242880 | tf_op jit(solution)/shard_map/mul | solution.py:36
  31.9 6.1 %mul.73 = f32[256,4096]{1,0:T(8,128)} reshape(f32[128,2,4096]{2,1,0:T(2,128)} %mul.72) | data formatting | bytes 8388608 | tf_op jit(solution)/shard_map/mul | solution.py:36
  38.0 0.1 copy.36
  38.1 0.1 mul.74
  38.2 4.6 %convolution_convert_fusion.2 = bf16[320,4096]{1,0:T(8,128)(2,1)} fusion(f32[256,4096]{1,0:T(8,128)} %mul.73, f32[256]{0:T(256)S(1)} %mul.74, s32[256]{0:T(256)S(1)} %get-tuple-element.15), kind=kOutput, calls=%fused_computation.4 | convolution fusion | flops 674578432 | bytes 6817792 | tf_op jit(solution)/shard_map/dot_general | solution.py:39
  42.9 4.3 %reshape.70 = bf16[16,20,4096]{2,1,0:T(8,128)(2,1)} reshape(bf16[320,4096]{1,0:T(8,128)(2,1)} %convolution_convert_fusion.2) | data formatting | bytes 5242880 | tf_op jit(solution)/shard_map/reshape | solution.py:49
  47.2 17.7 %all-to-all-done.1 = bf16[16,20,4096]{2,1,0:T(8,128)(2,1)} async-done(((bf16[16,20,4096]{2,1,0:T(8,128)(2,1)}), bf16[16,20,4096]{2,1,0:T(8,128)(2,1)}, u32[]{:S(2)}, u32[]{:S(2)}) %all-to-all-start.1) | async-done | bytes 2621472 | tf_op jit(solution)/shard_map/all_to_all | solution.py:41
  64.8 8.0 %all-to-all-start = ((bf16[16,20,4096]{2,1,0:T(8,128)(2,1)}), bf16[16,20,4096]{2,1,0:T(8,128)(2,1)}, u32[]{:S(2)}, u32[]{:S(2)}) async-start(bf16[16,20,4096]{2,1,0:T(8,128)(2,1)} %reshape.70), calls=%async_computation | async-start | bytes 6291456 | tf_op jit(solution)/shard_map/all_to_all | solution.py:48
  72.9 0.0 reduce-scatter.4.cloned.1.call-start
  72.9 0.0 copy-done.5
  72.9 0.1 broadcast_bitcast_fusion
  73.0 4.3 %reshape.73 = bf16[320,4096]{1,0:T(8,128)(2,1)} reshape(bf16[16,20,4096]{2,1,0:T(8,128)(2,1)} %all-to-all-done.1) | data formatting | bytes 5242880 | tf_op jit(solution)/shard_map/reshape | solution.py:56
  77.3 35.2 %all-to-all-done = bf16[16,20,4096]{2,1,0:T(8,128)(2,1)} async-done(((bf16[16,20,4096]{2,1,0:T(8,128)(2,1)}), bf16[16,20,4096]{2,1,0:T(8,128)(2,1)}, u32[]{:S(2)}, u32[]{:S(2)}) %all-to-all-start) | async-done | bytes 2621472 | tf_op jit(solution)/shard_map/all_to_all | solution.py:48
  112.5 4.3 %reshape.71 = bf16[320,4096]{1,0:T(8,128)(2,1)} reshape(bf16[16,20,4096]{2,1,0:T(8,128)(2,1)} %all-to-all-done) | data formatting | bytes 5242880 | tf_op jit(solution)/shard_map/reshape | solution.py:57
  116.8 3.4 %fusion.3 = f32[320,256]{1,0:T(8,128)S(1)} fusion(bf16[320,4096]{1,0:T(8,128)(2,1)} %reshape.73, bf16[4096,384]{1,0:T(8,128)(2,1)} %bitcast.30), kind=kOutput, calls=%fused_computation.9 | convolution fusion | flops 671088640 | bytes 5046272 | tf_op jit(solution)/shard_map/dot_general | solution.py:60
  120.2 0.0 copy-done.1
  120.2 2.1 multiply_convert_fusion.4
  122.3 0.8 fusion.10
  123.1 1.0 copy-done.2
  124.0 1.3 fusion.9
  125.3 2.4 fusion
  127.7 4.6 %copy.38 = bf16[4096,384]{1,0:T(8,128)(2,1)} copy(bf16[4096,384]{0,1:T(8,128)(2,1)} %fusion) | data formatting | bytes 6291456
  132.3 0.0 reduce-scatter.4.cloned.1.call-update
  132.4 4.1 %convolution_convert_fusion = bf16[320,4096]{1,0:T(8,128)(2,1)} fusion(bf16[4096,384]{1,0:T(8,128)(2,1)} %bitcast.32, bf16[320,128]{1,0:T(8,128)(2,1)S(1)} %get-tuple-element.13, bf16[320,128]{1,0:T(8,128)(2,1)S(1)} %get-tuple-element.12), kind=kOutput, calls=%fused_computation.2 | convolution fusion | flops 672727040 | bytes 4882432 | tf_op jit(solution)/shard_map/dot_general | solution.py:79
  136.4 4.3 %reshape.74 = bf16[16,20,4096]{2,1,0:T(8,128)(2,1)} reshape(bf16[320,4096]{1,0:T(8,128)(2,1)} %convolution_convert_fusion) | data formatting | bytes 5242880 | tf_op jit(solution)/shard_map/reshape | solution.py:87
  140.8 45.9 %all_to_all.15 = bf16[16,20,4096]{2,1,0:T(8,128)(2,1)} all-to-all(bf16[16,20,4096]{2,1,0:T(8,128)(2,1)} %reshape.74), channel_id=1, replica_groups=mesh['rep'=32,'exp'=16] {'exp'}, dimensions={0} | all-to-all | bytes 5242880 | tf_op jit(solution)/shard_map/all_to_all | solution.py:86
  186.6 4.3 %reshape.75 = bf16[320,4096]{1,0:T(8,128)(2,1)} reshape(bf16[16,20,4096]{2,1,0:T(8,128)(2,1)} %all_to_all.15) | data formatting | bytes 5242880 | tf_op jit(solution)/shard_map/reshape | solution.py:93
  190.9 3.5 %convolution_convert_fusion.3 = bf16[128,4096]{1,0:T(8,128)(2,1)} fusion(bf16[320,4096]{1,0:T(8,128)(2,1)} %reshape.75, s32[320,128]{1,0:T(8,128)S(1)} %convert_reduce_fusion), kind=kOutput, calls=%fused_computation.5 | convolution fusion | flops 336109568 | bytes 3833856 | tf_op jit(solution)/shard_map/dot_general | solution.py:13
  194.4 63.6 %reduce-scatter.4.cloned.1.call-done = bf16[128,384]{1,0:T(8,128)(2,1)} async-done(((bf16[4096,384]{1,0:T(8,128)(2,1)}), bf16[128,384]{1,0:T(8,128)(2,1)}) %reduce-scatter.4.cloned.1.call-update) | async-done | bytes 98320
  258.0 1.0 copy.39
  259.0 0.8 copy.37
  (14 shorter events, 0.1 us)
Async XLA Ops:
  7.2 3.7 %copy-start = (bf16[128,4096]{1,0:T(8,128)(2,1)S(1)}, bf16[128,4096]{1,0:T(8,128)(2,1)}, u32[]{:S(2)}) copy-start(bf16[128,4096]{1,0:T(8,128)(2,1)} %param.6) | copy-start | bytes 3145732
  7.2 109.6 %all-gather.3.cloned.1.call-start = ((), (), s32[]{:S(2)}) async-start(), calls=%async_computation.4 | async-start | bytes 3244032 | tf_op jit(solution)/shard_map/all_gather | solution.py:59
  17.6 10.2 %copy-start.3 = (bf16[128,4096]{1,0:T(8,128)(2,1)S(1)}, bf16[128,4096]{1,0:T(8,128)(2,1)}, u32[]{:S(2)}) copy-start(bf16[128,4096]{1,0:T(8,128)(2,1)} %param.7) | copy-start | bytes 3145732
  17.6 47.2 %all-to-all-start.1 = ((bf16[16,20,4096]{2,1,0:T(8,128)(2,1)}), bf16[16,20,4096]{2,1,0:T(8,128)(2,1)}, u32[]{:S(2)}, u32[]{:S(2)}) async-start(bf16[16,20,4096]{2,1,0:T(8,128)(2,1)} %reshape.72), calls=%async_computation.1 | async-start | bytes 6291456 | tf_op jit(solution)/shard_map/all_to_all | solution.py:41
  31.9 6.1 %copy-start.4 = (f32[128,2]{0,1:T(2,128)S(1)}, f32[128,2]{0,1:T(2,128)}, u32[]{:S(2)}) copy-start(f32[128,2]{0,1:T(2,128)} %param.8) | copy-start | bytes 3076
  47.2 25.7 %copy-start.5 = (s32[1,1,32]{2,1,0:T(1,128)S(1)}, s32[1,1,32]{2,1,0:T(1,128)}, u32[]{:S(2)}) copy-start(s32[1,1,32]{2,1,0:T(1,128)} %param.11) | copy-start | bytes 388
  64.8 47.7 %all-to-all-start = ((bf16[16,20,4096]{2,1,0:T(8,128)(2,1)}), bf16[16,20,4096]{2,1,0:T(8,128)(2,1)}, u32[]{:S(2)}, u32[]{:S(2)}) async-start(bf16[16,20,4096]{2,1,0:T(8,128)(2,1)} %reshape.70), calls=%async_computation | async-start | bytes 6291456 | tf_op jit(solution)/shard_map/all_to_all | solution.py:48
  72.9 185.1 %reduce-scatter.4.cloned.1.call-start = ((), (), s32[]{:S(2)}) async-start(), calls=%async_computation.5 | async-start | bytes 3244032
  116.8 3.4 %copy-start.1 = (bf16[320,4096]{1,0:T(8,128)(2,1)S(1)}, bf16[320,4096]{1,0:T(8,128)(2,1)}, u32[]{:S(2)}) copy-start(bf16[320,4096]{1,0:T(8,128)(2,1)} %reshape.71) | copy-start | bytes 7864324
  122.3 1.7 copy-start.2
Sparse Core Ops, SparseCore 0:
  10.1 76.7 all-gather.2
  132.5 125.4 reduce-scatter.3
where the time goes:
time: 268 us; the launch traced here: 267 us
  waiting for transfers between devices  117 us (44%)
  blocking collectives  45.9 us (17%)
  local copies, waits for them, and re-layouts  45.2 us (17%)
  matrix products  22.2 us (8%)
  starting transfers between devices  18.3 us (7%)
  between operations  14.2 us (5%)
  other arithmetic  3.85 us (1%)
    unnamed x3, waiting for transfers between devices  64.3 us
    all_to_all x1, blocking collectives, per_device(): lax.all_to_all(slot_grad.reshape(expert_count, capacity, model_width), 'e...  45.9 us
    all_to_all x1, waiting for transfers between devices, per_device(): lax.all_to_all(send_dy.reshape(expert_count, capacity, model_width), 'exp...  35.2 us
    all_to_all x1, waiting for transfers between devices, per_device(): lax.all_to_all(send_x.reshape(expert_count, capacity, model_width), 'exp'...  17.7 us
    mul x3, local copies, waits for them, and re-layouts, per_device(): grad_out.astype(jnp.float32)[:, None, :] * gates[:, :, None]  10.3 us
    all_to_all x1, starting transfers between devices, per_device(): lax.all_to_all(send_x.reshape(expert_count, capacity, model_width), 'exp'...  10.2 us
    unnamed x17, local copies, waits for them, and re-layouts  8.35 us
    all_to_all x1, starting transfers between devices, per_device(): lax.all_to_all(send_dy.reshape(expert_count, capacity, model_width), 'exp...  8 us
  transfers between devices with their start and end apart: 4, of which 3 were waited for; matrix products, arithmetic and copies ran while one was open for 20% of the time, Pallas kernels for 0%

commit v1 on v0

v1 whole, which is shorter than its diff:
```python
import functools

import jax
import jax.numpy as jnp
from jax import lax
from jax.experimental import pallas as pl
from jax.experimental.pallas import tpu as pltpu
from jax.sharding import PartitionSpec as P

BF16 = jnp.bfloat16
F32 = jnp.float32
TOK, WIDTH, EXPERTS, CAP, HID = 128, 4096, 16, 20, 128
HALF = WIDTH // 2
ROWS = 2 * EXPERTS * CAP
STEPS = 4
COLS = HALF // STEPS
BLOCKS = WIDTH // 128


def half_of_row(shape, axis):
    row = lax.broadcasted_iota(jnp.int32, shape, axis)
    group = (row * 1639) >> 16
    rest = row - group * (2 * CAP)
    upper = rest >= CAP
    return upper, group * CAP + jnp.where(upper, rest - CAP, rest)


def targets(ids):
    expert = lax.broadcasted_iota(jnp.int32, (EXPERTS, TOK), 0)
    first = (jnp.broadcast_to(ids[0:1, :], (EXPERTS, TOK)) == expert).astype(F32)
    second = (jnp.broadcast_to(ids[1:2, :], (EXPERTS, TOK)) == expert).astype(F32)
    earlier = lax.broadcasted_iota(jnp.int32, (TOK, TOK), 0) < lax.broadcasted_iota(
        jnp.int32, (TOK, TOK), 1
    )
    before = jnp.dot(
        (first + second).astype(BF16),
        earlier.astype(F32).astype(BF16),
        preferred_element_type=F32,
    )
    rank0 = jnp.sum(first * before, 0, keepdims=True).astype(jnp.int32)
    rank1 = jnp.sum(second * before, 0, keepdims=True).astype(jnp.int32)
    return ids[0:1, :] * CAP + rank0, ids[1:2, :] * CAP + rank1


def hits(ids):
    target0, target1 = targets(ids)
    upper, slot = half_of_row((ROWS, TOK), 0)
    hit0 = slot == jnp.broadcast_to(target0, (ROWS, TOK))
    hit1 = slot == jnp.broadcast_to(target1, (ROWS, TOK))
    return hit0, hit1, upper


def placement(hit0, hit1, upper):
    hit = jnp.where(hit0 | hit1, 1.0, 0.0)
    return jnp.concatenate([jnp.where(upper, 0.0, hit), jnp.where(upper, hit, 0.0)], 1)


def place_tokens_kernel(ids_ref, low_ref, high_ref, out_ref, place):
    @pl.when(pl.program_id(0) == 0)
    def _():
        place[...] = placement(*hits(ids_ref[...])).astype(BF16)

    both = jnp.concatenate([low_ref[...], high_ref[...]], 0)
    out_ref[...] = jnp.dot(place[...], both, preferred_element_type=F32).astype(BF16)


def place_grads_kernel(ids_ref, gates_ref, low_ref, high_ref, out_ref, back_ref, place, gate):
    @pl.when(pl.program_id(0) == 0)
    def _():
        hit0, hit1, upper = hits(ids_ref[...])
        where_to = placement(hit0, hit1, upper)
        place[...] = where_to.astype(BF16)
        back_ref[...] = where_to.T.astype(BF16)
        gates = gates_ref[...]
        weight = jnp.where(hit0, jnp.broadcast_to(gates[0:1, :], (ROWS, TOK)), 0.0) + jnp.where(
            hit1, jnp.broadcast_to(gates[1:2, :], (ROWS, TOK)), 0.0
        )
        gate[...] = jnp.broadcast_to(jnp.sum(weight, 1, keepdims=True), (ROWS, 128))

    both = jnp.concatenate([low_ref[...], high_ref[...]], 0)
    picked = jnp.dot(place[...], both, preferred_element_type=F32)
    scale = gate[...]
    for i in range(COLS // 128):
        out_ref[:, i * 128 : i * 128 + 128] = (picked[:, i * 128 : i * 128 + 128] * scale).astype(
            BF16
        )


def join_halves(acc, width):
    upper, _ = half_of_row((ROWS, width), 0)
    own = jnp.where(upper, acc[:, width:], acc[:, :width])
    other = jnp.where(upper, pltpu.roll(own, CAP, 0), pltpu.roll(own, ROWS - CAP, 0))
    return own + other


def gate_up_kernel(x_ref, w_low_ref, w_high_ref, out_ref, acc):
    k = pl.program_id(0)

    @pl.when(k == 0)
    def _():
        acc[...] = jnp.zeros_like(acc)

    x = x_ref[...]
    acc[:, : 2 * HID] += jnp.dot(x, w_low_ref[:, : 2 * HID], preferred_element_type=F32)
    acc[:, 2 * HID :] += jnp.dot(x, w_high_ref[:, : 2 * HID], preferred_element_type=F32)

    @pl.when(k == STEPS - 1)
    def _():
        out_ref[...] = join_halves(acc[...], 2 * HID)


def hidden_kernel(dy_ref, w_low_ref, w_high_ref, gu_ref, both_ref, turned_ref, acc):
    k = pl.program_id(0)

    @pl.when(k == 0)
    def _():
        acc[...] = jnp.zeros_like(acc)

    weights = jnp.concatenate([w_low_ref[...], w_high_ref[...]], 1)
    acc[...] += jnp.dot(dy_ref[...], weights, preferred_element_type=F32)

    @pl.when(k == STEPS - 1)
    def _():
        hid_grad = join_halves(acc[...], HID)
        gate_pre = gu_ref[:, :HID]
        up_pre = gu_ref[:, HID:]
        sigmoid_g = jax.nn.sigmoid(gate_pre)
        silu_val = gate_pre * sigmoid_g
        silu_slope = sigmoid_g * (1.0 + gate_pre * (1.0 - sigmoid_g))
        gate_grad = hid_grad * up_pre * silu_slope
        up_grad = hid_grad * silu_val
        hidden = silu_val * up_pre
        both_ref[:, :HID] = gate_grad.astype(BF16)
        both_ref[:, HID:] = up_grad.astype(BF16)
        upper, _ = half_of_row((HID, ROWS), 1)
        for i, value in enumerate((gate_grad, up_grad, hidden)):
            turned = value.T
            turned_ref[i * HID : (i + 1) * HID, :] = jnp.where(upper, 0.0, turned).astype(BF16)
            turned_ref[(i + 3) * HID : (i + 4) * HID, :] = jnp.where(upper, turned, 0.0).astype(
                BF16
            )


def weight_grad_kernel(info_ref, turned_ref, x_ref, dy_ref, mine_ref, other_ref):
    step = pl.program_id(0)
    core = info_ref[0]
    x = x_ref[...]
    dy = dy_ref[...]
    for h in range(2):
        base = 3 * HID * h
        proj = jnp.dot(turned_ref[base : base + 2 * HID, :], x, preferred_element_type=F32)
        down = jnp.dot(
            turned_ref[base + 2 * HID : base + 3 * HID, :], dy, preferred_element_type=F32
        )
        for i in range(COLS // 128):
            block = step * (COLS // 128) + i + h * (BLOCKS // 2)
            keep = info_ref[1 + block].astype(F32)
            place = step * (COLS // 256) + i // 2 + h * (BLOCKS // 4)
            top = (proj[:, i * 128 : i * 128 + 128] * keep).astype(BF16)
            bottom = (down[:, i * 128 : i * 128 + 128] * keep).astype(BF16)

            def put(ref):
                ref[place, : 2 * HID, :] = top
                ref[place, 2 * HID :, :] = bottom

            pl.when(core == i % 2)(functools.partial(put, mine_ref))
            pl.when(core != i % 2)(functools.partial(put, other_ref))


def slot_grad_kernel(both_ref, w_low_ref, w_high_ref, out_ref):
    both = both_ref[...]
    upper, _ = half_of_row((ROWS, 2 * HID), 0)
    zero = jnp.zeros_like(both)
    dims = (((1,), (1,)), ((), ()))
    low = lax.dot_general(
        jnp.where(upper, zero, both), w_low_ref[:, : 2 * HID], dims, preferred_element_type=F32
    )
    high = lax.dot_general(
        jnp.where(upper, both, zero), w_high_ref[:, : 2 * HID], dims, preferred_element_type=F32
    )
    out_ref[...] = (low + high).astype(BF16)


def combine_kernel(back_ref, slots_ref, out_ref):
    step = pl.program_id(0)
    total = jnp.dot(back_ref[...], slots_ref[...], preferred_element_type=F32).astype(BF16)
    at = pl.multiple_of(step * COLS, COLS)
    out_ref[:, pl.ds(at, COLS)] = total[:TOK, :]
    out_ref[:, pl.ds(pl.multiple_of(at + HALF, COLS), COLS)] = total[TOK:, :]


def whole(shape):
    return pl.BlockSpec(shape, lambda i: (0,) * len(shape))


def columns(rows, shift=0):
    return pl.BlockSpec((rows, COLS), lambda i: (0, i + shift))


def weight_rows(width, shift=0, column=0):
    return pl.BlockSpec((COLS, width), lambda i: (i + shift, column))


def call(kernel, ins, outs, shapes, flops, nbytes, scratch=()):
    return pl.pallas_call(
        kernel,
        grid=(STEPS,),
        in_specs=ins,
        out_specs=outs,
        out_shape=shapes,
        scratch_shapes=list(scratch),
        compiler_params=pltpu.CompilerParams(dimension_semantics=("arbitrary",)),
        cost_estimate=pl.CostEstimate(flops=flops, bytes_accessed=nbytes, transcendentals=0),
    )


def sds(shape, dtype):
    return jax.ShapeDtypeStruct(shape, dtype)


def exchange(rows):
    return lax.all_to_all(
        rows.reshape(EXPERTS, 2 * CAP, HALF), "exp", split_axis=0, concat_axis=0, tiled=True
    ).reshape(ROWS, HALF)


def per_device(tokens, grad_out, gates, expert_ids, w_all, touched):
    rep = lax.axis_index("rep")
    reps = lax.axis_size("rep")
    ids = expert_ids.T
    mbytes = 1 << 20
    send_x = call(
        place_tokens_kernel,
        [whole((2, TOK)), columns(TOK), columns(TOK, STEPS)],
        columns(ROWS),
        sds((ROWS, HALF), BF16),
        2 * ROWS * 256 * HALF,
        4 * mbytes,
        [pltpu.VMEM((ROWS, 2 * TOK), BF16)],
    )(ids, tokens, tokens)
    slot_x = exchange(send_x)
    send_dy, back = call(
        place_grads_kernel,
        [whole((2, TOK)), whole((2, TOK)), columns(TOK), columns(TOK, STEPS)],
        [columns(ROWS), whole((2 * TOK, ROWS))],
        [sds((ROWS, HALF), BF16), sds((2 * TOK, ROWS), BF16)],
        2 * ROWS * 256 * HALF,
        4 * mbytes,
        [pltpu.VMEM((ROWS, 2 * TOK), BF16), pltpu.VMEM((ROWS, 128), F32)],
    )(ids, gates.T, grad_out, grad_out)
    slot_dy = exchange(send_dy)
    w_whole = lax.all_gather(w_all[0], "rep", axis=0, tiled=True)
    gate_up = call(
        gate_up_kernel,
        [columns(ROWS), weight_rows(3 * HID), weight_rows(3 * HID, STEPS)],
        whole((ROWS, 2 * HID)),
        sds((ROWS, 2 * HID), F32),
        2 * ROWS * HALF * 4 * HID,
        6 * mbytes,
        [pltpu.VMEM((ROWS, 4 * HID), F32)],
    )(slot_x, w_whole, w_whole)
    both_grad, turned = call(
        hidden_kernel,
        [
            columns(ROWS),
            weight_rows(HID, 0, 2),
            weight_rows(HID, STEPS, 2),
            whole((ROWS, 2 * HID)),
        ],
        [whole((ROWS, 2 * HID)), whole((6 * HID, ROWS))],
        [sds((ROWS, 2 * HID), BF16), sds((6 * HID, ROWS), BF16)],
        2 * ROWS * HALF * 2 * HID,
        4 * mbytes,
        [pltpu.VMEM((ROWS, 2 * HID), F32)],
    )(slot_dy, w_whole, w_whole, gate_up)
    info = jnp.concatenate([jnp.reshape(rep % 2, (1,)), touched.reshape(-1)])
    share = (BLOCKS // 2, 3 * HID, 128)
    mine, other = call(
        weight_grad_kernel,
        [
            pl.BlockSpec(memory_space=pltpu.SMEM),
            whole((6 * HID, ROWS)),
            columns(ROWS),
            columns(ROWS),
        ],
        [whole(share), whole(share)],
        [sds(share, BF16), sds(share, BF16)],
        2 * ROWS * HALF * 6 * HID,
        8 * mbytes,
    )(info, turned, slot_x, slot_dy)
    swap = [(i, i ^ 1) for i in range(reps)]
    received = lax.ppermute(other, "rep", swap)
    paired = (mine.astype(F32) + received.astype(F32)).astype(BF16)
    owned = lax.psum_scatter(
        paired,
        "rep",
        scatter_dimension=0,
        axis_index_groups=[list(range(c, reps, 2)) for c in range(2)],
        tiled=True,
    )
    slot_grad = call(
        slot_grad_kernel,
        [whole((ROWS, 2 * HID)), weight_rows(3 * HID), weight_rows(3 * HID, STEPS)],
        columns(ROWS),
        sds((ROWS, HALF), BF16),
        2 * ROWS * HALF * 4 * HID,
        6 * mbytes,
    )(both_grad, w_whole, w_whole)
    returned = exchange(slot_grad)
    token_grad = call(
        combine_kernel,
        [whole((2 * TOK, ROWS)), columns(ROWS)],
        whole((TOK, WIDTH)),
        sds((TOK, WIDTH), BF16),
        2 * ROWS * 256 * HALF,
        4 * mbytes,
    )(back, returned)
    weight_grad = jnp.swapaxes(owned, 1, 2).astype(F32)
    return (token_grad, weight_grad)


def solution(mesh):
    in_specs = (
        P(("rep", "exp"), None),
        P(("rep", "exp"), None),
        P(("rep", "exp"), None),
        P(("rep", "exp"), None),
        P("exp", "rep", None),
        P("rep", "exp", None),
    )
    out_specs = (P(("rep", "exp"), None), P("exp", "rep", None))
    return jax.shard_map(
        per_device, mesh=mesh, in_specs=in_specs, out_specs=out_specs, check_vma=False
    )
```

time: 268 us -> 207 us (0.77)
  local copies, waits for them, and re-layouts: 45.2 us -> 2.32 us
  Pallas kernels: 0 us -> 38.3 us
  waiting for transfers between devices: 117 us -> 85.3 us
  matrix products: 22.2 us -> 0 us
  blocking collectives: 45.9 us -> 42.3 us
    unnamed x3 -> x2, waiting for transfers between devices: 64.3 us -> 0.7 us
    pallas_call x0 -> x7, Pallas kernels: none -> 38.3 us  [the longest x1 7.97 us: per_device(): call(weight_grad_kernel, [pl.BlockSpec(memory_space=pltpu.SMEM), whole((6...]
    reduce_scatter x0 -> x1, waiting for transfers between devices: none -> 28.4 us  [per_device(): lax.psum_scatter(paired, 'rep', scatter_dimension=0, axis_index_groups=[l...]
    reshape x6 -> x0, local copies, waits for them, and re-layouts: 25.8 us -> none  [the longest x1 4.32 us: per_device(): slot_grad.reshape(expert_count, capacity, model_width)]
    all_to_all x2, waiting for transfers between devices: 52.9 us -> 29.2 us  [exchange(): lax.all_to_all(rows.reshape(EXPERTS, 2 * CAP, HALF), 'exp', split_axis=0,...]
    all_gather x1, waiting for transfers between devices: 0.01 us -> 23.4 us  [per_device(): w_whole = lax.all_gather(w_all[0], 'rep', axis=0, tiled=True)]
    dot_general x8 -> x0, matrix products: 22.2 us -> none  [the longest x3 5.56 us: contract_rows(): lax.dot_general(left, right, (((0,), (0,)), ((), ())), preferred_element_...]
    mul x4 -> x0, local copies, waits for them, and re-layouts: 10.3 us -> none  [the longest x3 10.3 us: per_device(): grad_out.astype(jnp.float32)[:, None, :] * gates[:, :, None]]
  transfers between devices with their start and end apart: 4 -> 5, of which waited for: 3 -> 5; matrix products, arithmetic and copies ran while one was open for 20% -> 0% of each run, Pallas kernels for 0% -> 12%
where the time goes in v1:
time: 207 us; the launch traced here: 206 us
  waiting for transfers between devices  85.3 us (41%)
  blocking collectives  42.3 us (20%)
  Pallas kernels  38.3 us (19%)
  starting transfers between devices  19.5 us (9%)
  between operations  14.1 us (7%)
  other arithmetic  4.56 us (2%)
  local copies, waits for them, and re-layouts  2.32 us (1%)
    all_to_all x1, blocking collectives, exchange(): lax.all_to_all(rows.reshape(EXPERTS, 2 * CAP, HALF), 'exp', split_axis=0,...  42.3 us
    all_to_all x2, waiting for transfers between devices, exchange(): lax.all_to_all(rows.reshape(EXPERTS, 2 * CAP, HALF), 'exp', split_axis=0,...  29.2 us
    reduce_scatter x1, waiting for transfers between devices, per_device(): lax.psum_scatter(paired, 'rep', scatter_dimension=0, axis_index_groups=[l...  28.4 us
    all_gather x1, waiting for transfers between devices, per_device(): w_whole = lax.all_gather(w_all[0], 'rep', axis=0, tiled=True)  23.4 us
    all_to_all x2, starting transfers between devices, exchange(): lax.all_to_all(rows.reshape(EXPERTS, 2 * CAP, HALF), 'exp', split_axis=0,...  17.5 us
    pallas_call x1, Pallas kernels, per_device(): call(weight_grad_kernel, [pl.BlockSpec(memory_space=pltpu.SMEM), whole((6...  7.97 us
    pallas_call x1, Pallas kernels, per_device(): call(hidden_kernel, [columns(ROWS), weight_rows(HID, 0, 2), weight_rows(H...  5.49 us
    pallas_call x1, Pallas kernels, per_device(): call(gate_up_kernel, [columns(ROWS), weight_rows(3 * HID), weight_rows(3...  5.41 us
  transfers between devices with their start and end apart: 5, of which 5 were waited for; matrix products, arithmetic and copies ran while one was open for 0% of the time, Pallas kernels for 12%

profile of v1, /device:TPU:2, one launch (start us, length us, event | category | flops | bytes accessed | tf_op | source)
XLA Modules:
  0.0 206.4 jit_solution(17431657849504303782)
XLA Ops:
  7.2 0.0 all-gather.3.cloned.1.call-start
  7.2 0.7 all-gather.3.cloned.1.call-update
  7.9 4.8 %shard_map.78 = bf16[640,2048]{1,0:T(8,128)(2,1)} custom-call(s32[2,128]{1,0:T(2,128)} %bitcast.25, bf16[128,4096]{1,0:T(8,128)(2,1)} %high_ref.3, bf16[128,4096]{1,0:T(8,128)(2,1)} %high_ref.3), custom_call_target="tpu_custom_call" | custom-call | flops 671088640 | bytes 4194304 | tf_op jit(solution)/shard_map/pallas_call | solution.py:232
  12.7 9.4 %all-to-all-start.1 = ((bf16[16,40,2048]{2,1,0:T(8,128)(2,1)}), bf16[16,40,2048]{2,1,0:T(8,128)(2,1)S(1)}, u32[]{:S(2)}, u32[]{:S(2)}) async-start(bf16[16,40,2048]{2,1,0:T(8,128)(2,1)} %bitcast.21), calls=%async_computation.1 | async-start | bytes 5242880 | tf_op jit(solution)/shard_map/all_to_all | solution.py:222
  22.1 4.9 %shard_map.77 = (bf16[640,2048]{1,0:T(8,128)(2,1)}, bf16[256,640]{1,0:T(8,128)(2,1)}) custom-call(s32[2,128]{1,0:T(2,128)} %bitcast.26, f32[2,128]{1,0:T(2,128)} %bitcast.27, bf16[128,4096]{1,0:T(8,128)(2,1)} %high_ref.2, bf16[128,4096]{1,0:T(8,128)(2,1)} %high_ref.2), custom_call_target="tpu_custom_call" | custom-call | flops 671088640 | bytes 4194304 | tf_op jit(solution)/shard_map/pallas_call | solution.py:242
  27.0 26.2 %all-to-all-done.1 = bf16[16,40,2048]{2,1,0:T(8,128)(2,1)S(1)} async-done(((bf16[16,40,2048]{2,1,0:T(8,128)(2,1)}), bf16[16,40,2048]{2,1,0:T(8,128)(2,1)S(1)}, u32[]{:S(2)}, u32[]{:S(2)}) %all-to-all-start.1) | async-done | bytes 2621472 | tf_op jit(solution)/shard_map/all_to_all | solution.py:222
  53.3 0.0 copy-start
  53.3 0.0 copy-start.1
  53.3 1.5 copy-done
  54.8 8.1 %all-to-all-start = ((bf16[16,40,2048]{2,1,0:T(8,128)(2,1)}), bf16[16,40,2048]{2,1,0:T(8,128)(2,1)}, u32[]{:S(2)}, u32[]{:S(2)}) async-start(bf16[16,40,2048]{2,1,0:T(8,128)(2,1)} %bitcast.24), calls=%async_computation | async-start | bytes 5242880 | tf_op jit(solution)/shard_map/all_to_all | solution.py:222
  62.9 0.0 reduce-scatter.2.cloned.1.call-start
  62.9 0.0 copy-done.1
  62.9 0.7 pad_add_fusion.info_ref
  63.6 23.4 %all-gather.3.cloned.1.call-done = bf16[1,4096,384]{2,1,0:T(8,128)(2,1)} async-done(((bf16[1,128,384]{2,1,0:T(8,128)(2,1)}), bf16[1,4096,384]{2,1,0:T(8,128)(2,1)}) %all-gather.3.cloned.1.call-update) | async-done | bytes 3145744 | tf_op jit(solution)/shard_map/all_gather | solution.py:252
  87.0 5.4 %shard_map.79.gu_ref = f32[640,256]{1,0:T(8,128)} custom-call(bf16[640,2048]{1,0:T(8,128)(2,1)} %bitcast.19, bf16[4096,384]{1,0:T(8,128)(2,1)} %bitcast.13, bf16[4096,384]{1,0:T(8,128)(2,1)} %bitcast.14), custom_call_target="tpu_custom_call" | custom-call | flops 1342177280 | bytes 6291456 | tf_op jit(solution)/shard_map/pallas_call | solution.py:253
  92.4 3.0 %all-to-all-done = bf16[16,40,2048]{2,1,0:T(8,128)(2,1)} async-done(((bf16[16,40,2048]{2,1,0:T(8,128)(2,1)}), bf16[16,40,2048]{2,1,0:T(8,128)(2,1)}, u32[]{:S(2)}, u32[]{:S(2)}) %all-to-all-start) | async-done | bytes 2621472 | tf_op jit(solution)/shard_map/all_to_all | solution.py:222
  95.4 5.5 %shard_map.80 = (bf16[640,256]{1,0:T(8,128)(2,1)}, bf16[768,640]{1,0:T(8,128)(2,1)}) custom-call(bf16[640,2048]{1,0:T(8,128)(2,1)} %bitcast.3.dy_ref, bf16[4096,384]{1,0:T(8,128)(2,1)} %bitcast.15, bf16[4096,384]{1,0:T(8,128)(2,1)} %bitcast.16, f32[640,256]{1,0:T(8,128)} %shard_map.79.gu_ref), custom_call_target="tpu_custom_call" | custom-call | flops 671088640 | bytes 4194304 | tf_op jit(solution)/shard_map/pallas_call | solution.py:262
  100.9 8.0 %shard_map.83 = (bf16[16,384,128]{2,1,0:T(8,128)(2,1)}, bf16[16,384,128]{2,1,0:T(8,128)(2,1)}) custom-call(s32[33]{0:T(128)} %pad_add_fusion.info_ref, bf16[768,640]{1,0:T(8,128)(2,1)} %get-tuple-element.11.turned_ref, bf16[640,2048]{1,0:T(8,128)(2,1)} %bitcast.20, bf16[640,2048]{1,0:T(8,128)(2,1)} %bitcast.3.dy_ref), custom_call_target="tpu_custom_call" | custom-call | flops 2013265920 | bytes 8388608 | tf_op jit(solution)/shard_map/pallas_call | solution.py:278
  108.8 1.9 collective-permute-start
  110.8 3.6 %collective-permute-done = bf16[16,384,128]{2,1,0:T(8,128)(2,1)S(1)} collective-permute-done((bf16[16,384,128]{2,1,0:T(8,128)(2,1)}, bf16[16,384,128]{2,1,0:T(8,128)(2,1)S(1)}, u32[]{:S(2)}, u32[]{:S(2)}) %collective-permute-start) | collective-permute-done | bytes 1572896 | tf_op jit(solution)/shard_map/ppermute | solution.py:292
  114.3 3.0 %add_convert_fusion = bf16[16,384,128]{2,1,0:T(8,128)(2,1)} fusion(bf16[16,384,128]{2,1,0:T(8,128)(2,1)S(1)} %collective-permute-done, bf16[16,384,128]{2,1,0:T(8,128)(2,1)} %get-tuple-element.12), kind=kLoop, calls=%fused_computation | loop fusion | flops 3145728 | bytes 4718592 | tf_op jit(solution)/shard_map/convert_element_type | solution.py:293
  117.3 0.0 reduce-scatter.2.cloned.1.call-update
  117.4 5.3 %shard_map.81 = bf16[640,2048]{1,0:T(8,128)(2,1)} custom-call(bf16[640,256]{1,0:T(8,128)(2,1)} %get-tuple-element.10.both_ref, bf16[4096,384]{1,0:T(8,128)(2,1)} %bitcast.17, bf16[4096,384]{1,0:T(8,128)(2,1)} %bitcast.18), custom_call_target="tpu_custom_call" | custom-call | flops 1342177280 | bytes 6291456 | tf_op jit(solution)/shard_map/pallas_call | solution.py:301
  122.7 42.3 %all_to_all.15 = bf16[16,40,2048]{2,1,0:T(8,128)(2,1)} all-to-all(bf16[16,40,2048]{2,1,0:T(8,128)(2,1)} %bitcast.23), channel_id=1, replica_groups=mesh['rep'=32,'exp'=16] {'exp'}, dimensions={0} | all-to-all | bytes 5242880 | tf_op jit(solution)/shard_map/all_to_all | solution.py:222
  165.0 4.4 %shard_map.82 = bf16[128,4096]{1,0:T(8,128)(2,1)} custom-call(bf16[256,640]{1,0:T(8,128)(2,1)} %get-tuple-element.8.back_ref, bf16[640,2048]{1,0:T(8,128)(2,1)} %bitcast.22), custom_call_target="tpu_custom_call" | custom-call | flops 671088640 | bytes 4194304 | tf_op jit(solution)/shard_map/pallas_call | solution.py:310
  169.4 28.4 %reduce-scatter.2.cloned.1.call-done = bf16[1,384,128]{2,1,0:T(8,128)(2,1)} async-done(((bf16[16,384,128]{2,1,0:T(8,128)(2,1)}), bf16[1,384,128]{2,1,0:T(8,128)(2,1)}) %reduce-scatter.2.cloned.1.call-update) | async-done | bytes 98320 | tf_op jit(solution)/shard_map/reduce_scatter | solution.py:294
  197.9 0.9 convert_bitcast_fusion
  198.8 0.8 copy.8
Async XLA Ops:
  7.2 79.8 %all-gather.3.cloned.1.call-start = ((), (), s32[]{:S(2)}) async-start(), calls=%async_computation.5 | async-start | bytes 3244032 | tf_op jit(solution)/shard_map/all_gather | solution.py:252
  12.7 40.5 %all-to-all-start.1 = ((bf16[16,40,2048]{2,1,0:T(8,128)(2,1)}), bf16[16,40,2048]{2,1,0:T(8,128)(2,1)S(1)}, u32[]{:S(2)}, u32[]{:S(2)}) async-start(bf16[16,40,2048]{2,1,0:T(8,128)(2,1)} %bitcast.21), calls=%async_computation.1 | async-start | bytes 5242880 | tf_op jit(solution)/shard_map/all_to_all | solution.py:222
  53.3 1.5 copy-start
  53.3 9.7 %copy-start.1 = (s32[1,1,32]{2,1,0:T(1,128)S(1)}, s32[1,1,32]{2,1,0:T(1,128)}, u32[]{:S(2)}) copy-start(s32[1,1,32]{2,1,0:T(1,128)} %param.11) | copy-start | bytes 388
  54.8 40.6 %all-to-all-start = ((bf16[16,40,2048]{2,1,0:T(8,128)(2,1)}), bf16[16,40,2048]{2,1,0:T(8,128)(2,1)}, u32[]{:S(2)}, u32[]{:S(2)}) async-start(bf16[16,40,2048]{2,1,0:T(8,128)(2,1)} %bitcast.24), calls=%async_computation | async-start | bytes 5242880 | tf_op jit(solution)/shard_map/all_to_all | solution.py:222
  62.9 135.0 %reduce-scatter.2.cloned.1.call-start = ((), (), s32[]{:S(2)}) async-start(), calls=%async_computation.4 | async-start | bytes 1671168 | tf_op jit(solution)/shard_map/reduce_scatter | solution.py:294
  108.8 5.5 %collective-permute-start = (bf16[16,384,128]{2,1,0:T(8,128)(2,1)}, bf16[16,384,128]{2,1,0:T(8,128)(2,1)S(1)}, u32[]{:S(2)}, u32[]{:S(2)}) collective-permute-start(bf16[16,384,128]{2,1,0:T(8,128)(2,1)} %get-tuple-element.13), channel_id=1, source_target_pairs={{0,16},{16,0},{32,48},{48,32},{64,80},{80,64},{96,112},{112,96},{1... | collective-permute-start | bytes 4718600 | tf_op jit(solution)/shard_map/ppermute | solution.py:292
Sparse Core Ops, SparseCore 0:
  10.1 76.8 all-gather.2
  117.5 80.3 reduce-scatter.1
